TPU v7x, 32 devices: a whole 2x2x4 slice. The times are simulated.
32 devices in a mesh: group: 4 (over y, x), dp: 2 (over core), tensor: 4 (over z).
Axes of the slice: x: 2, y: 2, z: 4, core: 2. Of those that a mesh axis runs over, the one named last changes fastest.
Arguments:
- tokens: bfloat16 [8192, 2048], P(('group', 'dp')), may hold values from -6 to 6
- norm_gain: bfloat16 [2048], replicated, may hold values from 0.099609375 to 1.8984375
- w_query: bfloat16 [2048, 2048], P(None, 'tensor'), may hold values from -0.25 to 0.25
- w_keyval: bfloat16 [2048, 512], P(None, 'tensor'), may hold values from -0.125 to 0.125
- w_out: bfloat16 [2048, 2048], P('tensor'), may hold values from -0.8984375 to 0.8984375
- kv_cache: bfloat16 [4, 32, 16, 128, 512], P(None, ('group', 'dp'), None, None, 'tensor'), may hold values from -400 to 400
- lengths: int32 [32, 2], P(('group', 'dp')), may hold values from 0 to 2048, as said below
- dest_slot: int32 [32, 16], replicated, may hold values from 0 to 511, as said below
Outputs:
- mixed: bfloat16 [8192, 2048], P(('group', 'dp', 'tensor'))
- decode_cache: bfloat16 [4, 512, 128, 512], P(None, ('group', 'dp'), None, 'tensor')
Inputs may be any that keep to these rules, and one draw needn't show every extreme that they name: lengths[p, 0] lies in 0 to 2048 and lengths[p, 1] in 1 to 256; 2048 and 256 are each taken by some prompt; the prompts r * 4 to r * 4 + 3 of each index r of group and dp together hold exactly 32 live blocks. dest_slot is a permutation of the 512 slots; the slots of the index r of group and dp together are r * 4 * 16 onward; the blocks of prompts r * 4 to r * 4 + 3 send exactly 8 blocks to each index, of which exactly 4 is live.
All inputs are finite; a program needn't handle non-finite values.
Results may differ from a plain program's by a relative error of at most 0.009.
Values may be sent and summed in bfloat16 or wider, within the bound.
A program may use at most 128 MiB of HBM per device.

v0:
```python
import jax
import jax.numpy as jnp
from jax import lax
from jax.sharding import PartitionSpec as P

HD = 64


def per_device(tokens, norm_gain, w_query, w_keyval, w_out, kv_cache, lengths, dest_slot):
    tok_rows = tokens.shape[0]
    prompts = lengths.shape[0]
    fresh_rows = tok_rows // prompts
    heads_local = w_query.shape[1] // HD
    kv_local = w_keyval.shape[1] // (2 * HD)
    group_size = heads_local // kv_local
    layers = kv_cache.shape[0]
    blocks_win = kv_cache.shape[2]
    block_len = kv_cache.shape[3]
    lane_width = kv_cache.shape[4]
    window = blocks_win * block_len
    tokens_f = tokens.astype(jnp.float32)
    normed = (
        tokens_f
        * lax.rsqrt(jnp.mean(tokens_f * tokens_f, axis=-1, keepdims=True) + 1e-05)
        * norm_gain.astype(jnp.float32)
    ).astype(jnp.bfloat16)
    query = jnp.dot(normed, w_query, preferred_element_type=jnp.float32).astype(jnp.bfloat16)
    query = query.reshape(prompts, fresh_rows, kv_local, group_size, HD)
    keyval = jnp.dot(normed, w_keyval, preferred_element_type=jnp.float32).astype(jnp.bfloat16)
    keyval = keyval.reshape(prompts, fresh_rows, kv_local, 2, HD)
    cache = kv_cache[0].reshape(prompts, window, kv_local, 2, HD)
    scale = 1.0 / HD**0.5
    query_pos = jnp.arange(fresh_rows)[:, None]
    key_pos = jnp.arange(window + fresh_rows)[None, :]

    def attend(items):
        query_p, cache_p, fresh_p, history, fresh_len = items
        pairs = jnp.concatenate([cache_p, fresh_p], axis=0)
        scores = (
            jnp.einsum(
                "ckgd,tkd->kgct", query_p, pairs[:, :, 0], preferred_element_type=jnp.float32
            )
            * scale
        )
        visible = jnp.where(
            key_pos < window,
            (key_pos >= window - history) & (key_pos >= query_pos + 1),
            key_pos - window <= query_pos,
        )
        scores = jnp.where(visible, scores, -1e30)
        scores = scores - jnp.max(scores, axis=-1, keepdims=True)
        expo = jnp.exp(scores)
        weights = (expo / jnp.sum(expo, axis=-1, keepdims=True)).astype(jnp.bfloat16)
        mixed_p = jnp.einsum(
            "kgct,tkd->ckgd", weights, pairs[:, :, 1], preferred_element_type=jnp.float32
        )
        mixed_p = mixed_p.astype(jnp.bfloat16).reshape(fresh_rows, heads_local * HD)
        return jnp.where(
            (jnp.arange(fresh_rows) < fresh_len)[:, None], mixed_p, jnp.zeros_like(mixed_p)
        )

    attn = lax.map(attend, (query, cache, keyval, lengths[:, 0], lengths[:, 1]))
    attn = attn.reshape(tok_rows, heads_local * HD)
    mixed = lax.psum_scatter(
        jnp.dot(attn, w_out, preferred_element_type=jnp.float32),
        "tensor",
        scatter_dimension=0,
        tiled=True,
    ).astype(jnp.bfloat16)
    per_dev = prompts * blocks_win
    devices = lax.axis_size(("group", "dp"))
    per_peer = per_dev // devices
    my_index = lax.axis_index(("group", "dp"))
    dest_all = dest_slot.reshape(devices, per_dev)
    recv_all = dest_all // per_dev
    same_dest = recv_all[:, :, None] == recv_all[:, None, :]
    earlier = jnp.arange(per_dev)[None, :] < jnp.arange(per_dev)[:, None]
    own_recv = lax.dynamic_index_in_dim(recv_all, my_index, 0, keepdims=False)
    senders = jnp.arange(devices, dtype=jnp.int32)[:, None]
    capacity = per_peer // 2
    lengths_every = lax.all_gather(lengths, ("group", "dp"), axis=0, tiled=True)
    live_all = (
        (jnp.arange(blocks_win)[None, :] + 1) * block_len > window - lengths_every[:, 0:1]
    ).reshape(devices, per_dev)
    live_rank = jnp.sum(same_dest & earlier[None, :, :] & live_all[:, None, :], axis=2)
    own_live = lax.dynamic_index_in_dim(live_all, my_index, 0, keepdims=False)
    own_live_rank = lax.dynamic_index_in_dim(live_rank, my_index, 0, keepdims=False)
    send_pos = jnp.where(own_live, own_recv * capacity + own_live_rank, devices * capacity)
    send_idx = (
        jnp.zeros((devices * capacity,), jnp.int32)
        .at[send_pos]
        .set(jnp.arange(per_dev, dtype=jnp.int32), mode="drop")
    )
    raw_blocks = kv_cache.reshape(layers, per_dev, block_len, lane_width)
    outgoing = jnp.take(raw_blocks, send_idx, axis=1)
    incoming = lax.all_to_all(outgoing, ("group", "dp"), split_axis=1, concat_axis=1, tiled=True)
    where_from = senders * capacity + live_rank
    valid = (recv_all == my_index) & live_all
    slot_local = jnp.where(valid, dest_all - my_index * per_dev, per_dev)
    source_idx = (
        jnp.full((per_dev,), devices * capacity, jnp.int32)
        .at[slot_local.reshape(-1)]
        .set(where_from.reshape(-1), mode="drop")
    )
    decode_cache = jnp.take(incoming, source_idx, axis=1, mode="fill", fill_value=0)
    return (mixed, decode_cache)


def solution(mesh):
    in_specs = (
        P(("group", "dp"), None),
        P(),
        P(None, "tensor"),
        P(None, "tensor"),
        P("tensor", None),
        P(None, ("group", "dp"), None, None, "tensor"),
        P(("group", "dp"), None),
        P(),
    )
    out_specs = (P(("group", "dp", "tensor"), None), P(None, ("group", "dp"), None, "tensor"))
    return jax.shard_map(
        per_device, mesh=mesh, in_specs=in_specs, out_specs=out_specs, check_vma=False
    )
```

profile of v0, /device:TPU:0, one launch (start us, length us, event | category | flops | bytes accessed | tf_op | source)
XLA Modules:
  0.0 344.5 jit_solution(16174500329635103676)
XLA Ops:
  7.2 1.4 slice_bitcast_fusion
  8.6 3.2 slice.25
  11.8 4.5 %copy.51 = bf16[1,4,16,128,128]{3,2,4,1,0:T(8,128)(2,1)} copy(bf16[1,4,16,128,128]{4,3,2,1,0:T(8,128)(2,1)} %slice.25) | data formatting | bytes 4194304 | tf_op jit(solution)/shard_map/slice | solution.py:31
  16.3 4.2 %reshape_squeeze.3 = bf16[4,2048,1,2,64]{1,4,3,2,0:T(8,128)(2,1)} reshape(bf16[1,4,16,128,128]{3,2,4,1,0:T(8,128)(2,1)} %copy.51) | data formatting | bytes 4194304 | tf_op jit(solution)/shard_map/reshape;squeeze | solution.py:31
  20.4 3.1 fusion.27
  23.5 3.6 %fusion.33 = bf16[1024,128]{1,0:T(8,128)(2,1)S(1)} fusion(bf16[2048,128]{1,0:T(8,128)(2,1)} %param.13, bf16[1024,2048]{1,0:T(8,128)(2,1)} %param.10, f32[2048]{0:T(1024)S(1)} %convert_element_type.40, f32[1024]{0:T(1024)S(1)} %add_rsqrt_fusion), kind=kOutput, calls=%fused_computation.51 | convolution fusion | flops 545390592 | bytes 4993024 | tf_op jit(solution)/shard_map/dot_general | solution.py:29
  27.7 5.3 %convolution_convert_fusion = bf16[1024,512]{1,0:T(8,128)(2,1)S(1)} fusion(bf16[2048,512]{1,0:T(8,128)(2,1)} %param.12, bf16[1024,2048]{1,0:T(8,128)(2,1)} %param.10, f32[2048]{0:T(1024)S(1)} %convert_element_type.40, f32[1024]{0:T(1024)S(1)} %add_rsqrt_fusion), kind=kOutput, calls=%fused_computation.49 | convolution fusion | flops 2156396544 | bytes 7352320 | tf_op jit(solution)/shard_map/dot_general | solution.py:27
  33.0 2.1 reshape.481
  35.1 3.0 copy.55
  38.1 142.6 %while.14 = (s32[]{:T(128)}, bf16[4,256,512]{2,1,0:T(8,128)(2,1)}, s32[4]{0:T(128)}, bf16[4,2048,1,2,64]{1,4,3,2,0:T(8,128)(2,1)}, bf16[4,256,1,2,64]{1,4,3,2,0:...) while((s32[]{:T(128)}, bf16[4,256,512]{2,1,0:T(8,128)(2,1)}, ...), condition=%wide.region_4.5_spmd.clone.clone, body=%wide.region_1.4_spmd.clone.clone.sunk | while | flops 1268387072 | bytes 63510268 | solution.py:62
  38.1 1.3 dynamic_slice.91
  40.1 2.0 fusion.58
  42.2 1.1 dynamic-slice_bitcast_fusion.5
  43.3 9.0 %fusion.59 = (f32[8,256]{1,0:T(8,128)S(1)}, f32[2304,256,8]{1,0,2:T(8,128)}) fusion(pred[256,2304]{0,1:T(8,128)(4,1)S(1)} %fusion.58, bf16[4,256,1,8,64]{1,4,3,2,0:T(8,128)(2,1)} %get-tuple-element.310, s32[]{:T(128)S(6)} %copy.74, bf16[256,1,2,64]{0,3,2,1:T(8,128)(2,1)S(1)} %dynamic-slice_bitcast_fusion.4, ...), kind=kOutput, calls=%fused_computation.10.clone.1 | convolution fusion | flops 618723328 | bytes 20324356 | tf_op jit(solution)/shard_map/while/body/eval_jaxpr/ckgd,tkd->kgct/dot_general | solution.py:40
  52.3 10.2 %fusion.60 = f32[8,256]{1,0:T(8,128)S(1)} fusion(f32[2304,256,8]{1,0,2:T(8,128)} %get-tuple-element.284, f32[8,256]{1,0:T(8,128)S(1)} %get-tuple-element.285, pred[256,2304]{0,1:T(8,128)(4,1)S(1)} %fusion.58), kind=kLoop, calls=%fused_computation.9.clone.1 | loop fusion | flops 18872320 | bytes 19480576 | tf_op jit(solution)/shard_map/while/body/eval_jaxpr/reduce_sum | solution.py:53
  62.5 9.0 %fusion.61 = bf16[64,8,256]{2,0,1:T(8,128)(2,1)S(1)} fusion(f32[8,256]{1,0:T(8,128)S(1)} %fusion.60, f32[8,256]{1,0:T(8,128)S(1)} %get-tuple-element.285, f32[2304,256,8]{1,0,2:T(8,128)} %get-tuple-element.284, pred[256,2304]{0,1:T(8,128)(4,1)S(1)} %fusion.58, bf16[2048,1,2,64]{0,3,2,1:T(8,128)(2,1)S(1)} %dynamic-slice_bitcast_fusion.5, ...), kind=kOutput, calls=%fused_computation.17.clone.1 | convolution fusion | flops 628293632 | bytes 20332544 | tf_op jit(solution)/shard_map/while/body/eval_jaxpr/kgct,tkd->ckgd/dot_general | solution.py:54
  73.8 1.3 dynamic_slice.91
  75.8 2.0 fusion.58
  77.9 1.1 dynamic-slice_bitcast_fusion.5
  78.9 9.0 %fusion.59 = (f32[8,256]{1,0:T(8,128)S(1)}, f32[2304,256,8]{1,0,2:T(8,128)}) fusion(pred[256,2304]{0,1:T(8,128)(4,1)S(1)} %fusion.58, bf16[4,256,1,8,64]{1,4,3,2,0:T(8,128)(2,1)} %get-tuple-element.310, s32[]{:T(128)S(6)} %copy.74, bf16[256,1,2,64]{0,3,2,1:T(8,128)(2,1)S(1)} %dynamic-slice_bitcast_fusion.4, ...), kind=kOutput, calls=%fused_computation.10.clone.1 | convolution fusion | flops 618723328 | bytes 20324356 | tf_op jit(solution)/shard_map/while/body/eval_jaxpr/ckgd,tkd->kgct/dot_general | solution.py:40
  87.9 10.2 %fusion.60 = f32[8,256]{1,0:T(8,128)S(1)} fusion(f32[2304,256,8]{1,0,2:T(8,128)} %get-tuple-element.284, f32[8,256]{1,0:T(8,128)S(1)} %get-tuple-element.285, pred[256,2304]{0,1:T(8,128)(4,1)S(1)} %fusion.58), kind=kLoop, calls=%fused_computation.9.clone.1 | loop fusion | flops 18872320 | bytes 19480576 | tf_op jit(solution)/shard_map/while/body/eval_jaxpr/reduce_sum | solution.py:53
  98.1 9.0 %fusion.61 = bf16[64,8,256]{2,0,1:T(8,128)(2,1)S(1)} fusion(f32[8,256]{1,0:T(8,128)S(1)} %fusion.60, f32[8,256]{1,0:T(8,128)S(1)} %get-tuple-element.285, f32[2304,256,8]{1,0,2:T(8,128)} %get-tuple-element.284, pred[256,2304]{0,1:T(8,128)(4,1)S(1)} %fusion.58, bf16[2048,1,2,64]{0,3,2,1:T(8,128)(2,1)S(1)} %dynamic-slice_bitcast_fusion.5, ...), kind=kOutput, calls=%fused_computation.17.clone.1 | convolution fusion | flops 628293632 | bytes 20332544 | tf_op jit(solution)/shard_map/while/body/eval_jaxpr/kgct,tkd->ckgd/dot_general | solution.py:54
  109.5 1.3 dynamic_slice.91
  111.4 2.0 fusion.58
  113.5 1.1 dynamic-slice_bitcast_fusion.5
  114.6 9.0 %fusion.59 = (f32[8,256]{1,0:T(8,128)S(1)}, f32[2304,256,8]{1,0,2:T(8,128)}) fusion(pred[256,2304]{0,1:T(8,128)(4,1)S(1)} %fusion.58, bf16[4,256,1,8,64]{1,4,3,2,0:T(8,128)(2,1)} %get-tuple-element.310, s32[]{:T(128)S(6)} %copy.74, bf16[256,1,2,64]{0,3,2,1:T(8,128)(2,1)S(1)} %dynamic-slice_bitcast_fusion.4, ...), kind=kOutput, calls=%fused_computation.10.clone.1 | convolution fusion | flops 618723328 | bytes 20324356 | tf_op jit(solution)/shard_map/while/body/eval_jaxpr/ckgd,tkd->kgct/dot_general | solution.py:40
  123.6 10.2 %fusion.60 = f32[8,256]{1,0:T(8,128)S(1)} fusion(f32[2304,256,8]{1,0,2:T(8,128)} %get-tuple-element.284, f32[8,256]{1,0:T(8,128)S(1)} %get-tuple-element.285, pred[256,2304]{0,1:T(8,128)(4,1)S(1)} %fusion.58), kind=kLoop, calls=%fused_computation.9.clone.1 | loop fusion | flops 18872320 | bytes 19480576 | tf_op jit(solution)/shard_map/while/body/eval_jaxpr/reduce_sum | solution.py:53
  133.8 9.0 %fusion.61 = bf16[64,8,256]{2,0,1:T(8,128)(2,1)S(1)} fusion(f32[8,256]{1,0:T(8,128)S(1)} %fusion.60, f32[8,256]{1,0:T(8,128)S(1)} %get-tuple-element.285, f32[2304,256,8]{1,0,2:T(8,128)} %get-tuple-element.284, pred[256,2304]{0,1:T(8,128)(4,1)S(1)} %fusion.58, bf16[2048,1,2,64]{0,3,2,1:T(8,128)(2,1)S(1)} %dynamic-slice_bitcast_fusion.5, ...), kind=kOutput, calls=%fused_computation.17.clone.1 | convolution fusion | flops 628293632 | bytes 20332544 | tf_op jit(solution)/shard_map/while/body/eval_jaxpr/kgct,tkd->ckgd/dot_general | solution.py:54
  145.1 1.3 dynamic_slice.91
  147.1 2.0 fusion.58
  149.2 1.1 dynamic-slice_bitcast_fusion.5
  150.2 9.0 %fusion.59 = (f32[8,256]{1,0:T(8,128)S(1)}, f32[2304,256,8]{1,0,2:T(8,128)}) fusion(pred[256,2304]{0,1:T(8,128)(4,1)S(1)} %fusion.58, bf16[4,256,1,8,64]{1,4,3,2,0:T(8,128)(2,1)} %get-tuple-element.310, s32[]{:T(128)S(6)} %copy.74, bf16[256,1,2,64]{0,3,2,1:T(8,128)(2,1)S(1)} %dynamic-slice_bitcast_fusion.4, ...), kind=kOutput, calls=%fused_computation.10.clone.1 | convolution fusion | flops 618723328 | bytes 20324356 | tf_op jit(solution)/shard_map/while/body/eval_jaxpr/ckgd,tkd->kgct/dot_general | solution.py:40
  159.2 10.2 %fusion.60 = f32[8,256]{1,0:T(8,128)S(1)} fusion(f32[2304,256,8]{1,0,2:T(8,128)} %get-tuple-element.284, f32[8,256]{1,0:T(8,128)S(1)} %get-tuple-element.285, pred[256,2304]{0,1:T(8,128)(4,1)S(1)} %fusion.58), kind=kLoop, calls=%fused_computation.9.clone.1 | loop fusion | flops 18872320 | bytes 19480576 | tf_op jit(solution)/shard_map/while/body/eval_jaxpr/reduce_sum | solution.py:53
  169.4 9.0 %fusion.61 = bf16[64,8,256]{2,0,1:T(8,128)(2,1)S(1)} fusion(f32[8,256]{1,0:T(8,128)S(1)} %fusion.60, f32[8,256]{1,0:T(8,128)S(1)} %get-tuple-element.285, f32[2304,256,8]{1,0,2:T(8,128)} %get-tuple-element.284, pred[256,2304]{0,1:T(8,128)(4,1)S(1)} %fusion.58, bf16[2048,1,2,64]{0,3,2,1:T(8,128)(2,1)S(1)} %dynamic-slice_bitcast_fusion.5, ...), kind=kOutput, calls=%fused_computation.17.clone.1 | convolution fusion | flops 628293632 | bytes 20332544 | tf_op jit(solution)/shard_map/while/body/eval_jaxpr/kgct,tkd->ckgd/dot_general | solution.py:54
  180.8 6.8 %fusion.45 = f32[1024,2048]{1,0:T(8,128)} fusion(bf16[1024,512]{1,0:T(8,128)(2,1)} %bitcast.102, bf16[512,2048]{1,0:T(8,128)(2,1)S(1)} %copy-done), kind=kOutput, calls=%fused_computation.92 | convolution fusion | flops 2147483648 | bytes 11534336 | tf_op jit(solution)/shard_map/dot_general | solution.py:65
  187.8 10.3 %all-gather = s32[8,4,2]{1,2,0:T(2,128)S(1)} all-gather(s32[1,4,2]{1,2,0:T(2,128)S(1)} %bitcast.100), channel_id=1, replica_groups=mesh['group'=4,'dp'=2,'tensor'=4] {'group','dp'}, dimensions={0}, use_global_device_ids=true | all-gather | bytes 288 | tf_op jit(solution)/shard_map/all_gather | solution.py:81
  199.0 1.0 scatter_custom_fusion.1
  200.0 6.5 %gather_fusion = bf16[32,4,128,128]{3,2,1,0:T(8,128)(2,1)} fusion(bf16[4,64,128,128]{3,2,1,0:T(8,128)(2,1)} %bitcast.99, s32[1024]{0:T(1024)S(1)} %pad_clamp_fusion.1), kind=kCustom, calls=%fused_computation | custom fusion | bytes 8388736 | tf_op jit(solution)/shard_map/jit(_take)/gather | solution.py:95
  206.5 4.7 %select_bitcast_fusion.1 = bf16[4,32,128,128]{3,2,0,1:T(8,128)(2,1)} fusion(bf16[32,4,128,128]{3,2,1,0:T(8,128)(2,1)} %gather_fusion, pred[32]{0:T(512)(128)(4,1)S(1)} %compare_and_fusion), kind=kLoop, calls=%fused_computation.48 | loop fusion | flops 2097152 | bytes 8388640 | tf_op jit(solution)/shard_map/jit(_take)/select_n | solution.py:95
  211.1 4.6 %all-to-all-start = ((bf16[4,32,128,128]{3,2,0,1:T(8,128)(2,1)}), bf16[4,32,128,128]{3,2,0,1:T(8,128)(2,1)}, u32[]{:S(2)}, u32[]{:S(2)}) async-start(bf16[4,32,128,128]{3,2,0,1:T(8,128)(2,1)} %select_bitcast_fusion.1), calls=%async_computation.1 | async-start | bytes 8388608 | tf_op jit(solution)/shard_map/all_to_all | solution.py:96
  216.2 2.4 scatter_custom_fusion
  218.7 46.2 %all-to-all-done = bf16[4,32,128,128]{3,2,0,1:T(8,128)(2,1)} async-done(((bf16[4,32,128,128]{3,2,0,1:T(8,128)(2,1)}), bf16[4,32,128,128]{3,2,0,1:T(8,128)(2,1)}, u32[]{:S(2)}, u32[]{:S(2)}) %all-to-all-start) | async-done | bytes 4194336 | tf_op jit(solution)/shard_map/all_to_all | solution.py:96
  264.9 4.7 %copy.60 = bf16[4,32,128,128]{3,2,1,0:T(8,128)(2,1)} copy(bf16[4,32,128,128]{3,2,0,1:T(8,128)(2,1)} %all-to-all-done) | data formatting | bytes 8388608 | tf_op jit(solution)/shard_map/all_to_all | solution.py:96
  269.6 7.8 %gather_fusion.1 = bf16[64,4,128,128]{3,2,1,0:T(8,128)(2,1)} fusion(bf16[4,32,128,128]{3,2,1,0:T(8,128)(2,1)} %copy.60, s32[1024]{0:T(1024)S(1)} %pad_clamp_fusion), kind=kCustom, calls=%fused_computation.1 | custom fusion | bytes 16777472 | tf_op jit(solution)/shard_map/jit(_take)/gather | solution.py:105
  277.4 7.3 %select_bitcast_fusion = bf16[4,64,128,128]{3,2,0,1:T(8,128)(2,1)} fusion(bf16[64,4,128,128]{3,2,1,0:T(8,128)(2,1)} %gather_fusion.1, pred[64]{0:T(512)(128)(4,1)S(1)} %compare_and_fusion.1), kind=kLoop, calls=%fused_computation.47 | loop fusion | flops 4194304 | bytes 16777280 | tf_op jit(solution)/shard_map/jit(_take)/select_n | solution.py:105
  284.7 10.5 %copy.61 = bf16[4,64,128,128]{3,2,1,0:T(8,128)(2,1)} copy(bf16[4,64,128,128]{3,2,0,1:T(8,128)(2,1)} %select_bitcast_fusion) | data formatting | bytes 16777216
  295.2 39.7 %reduce-scatter.2.cloned.1.call-done = f32[256,2048]{1,0:T(8,128)} async-done(((f32[1024,2048]{1,0:T(8,128)}), f32[256,2048]{1,0:T(8,128)}) %reduce-scatter.2.cloned.1.call-update) | async-done | bytes 2097168 | tf_op jit(solution)/shard_map/reduce_scatter | solution.py:64
  334.9 2.7 convert_element_type.44
  (90 shorter events, 11.3 us)
Async XLA Ops:
  7.2 173.6 %copy-start = (bf16[512,2048]{1,0:T(8,128)(2,1)S(1)}, bf16[512,2048]{1,0:T(8,128)(2,1)}, u32[]{:S(2)}) copy-start(bf16[512,2048]{1,0:T(8,128)(2,1)} %param.14) | copy-start | bytes 6291460
  7.2 13.2 %copy-start.2 = (bf16[2048]{0:T(1024)(128)(2,1)S(1)}, bf16[2048]{0:T(1024)(128)(2,1)}, u32[]{:S(2)}) copy-start(bf16[2048]{0:T(1024)(128)(2,1)} %param.11) | copy-start | bytes 12292
  7.2 327.7 %reduce-scatter.2.cloned.1.call-start = ((), (), s32[]{:S(2)}) async-start(), calls=%async_computation.2 | async-start | bytes 10485760 | tf_op jit(solution)/shard_map/reduce_scatter | solution.py:64
  62.4 9.1 %copy-start.4 = (s32[4]{0:T(128)S(1)}, s32[4]{0:T(128)}, u32[]{:S(2)}) copy-start(s32[4]{0:T(128)} %get-tuple-element.306) | copy-start | bytes 52 | tf_op jit(solution)/shard_map/while
  98.1 9.1 %copy-start.4 = (s32[4]{0:T(128)S(1)}, s32[4]{0:T(128)}, u32[]{:S(2)}) copy-start(s32[4]{0:T(128)} %get-tuple-element.306) | copy-start | bytes 52 | tf_op jit(solution)/shard_map/while
  133.8 9.1 %copy-start.4 = (s32[4]{0:T(128)S(1)}, s32[4]{0:T(128)}, u32[]{:S(2)}) copy-start(s32[4]{0:T(128)} %get-tuple-element.306) | copy-start | bytes 52 | tf_op jit(solution)/shard_map/while
  169.4 9.1 %copy-start.4 = (s32[4]{0:T(128)S(1)}, s32[4]{0:T(128)}, u32[]{:S(2)}) copy-start(s32[4]{0:T(128)} %get-tuple-element.306) | copy-start | bytes 52 | tf_op jit(solution)/shard_map/while
  180.8 6.8 %copy-start.1 = (s32[32,16]{0,1:T(8,128)S(1)}, s32[32,16]{0,1:T(8,128)}, u32[]{:S(2)}) copy-start(s32[32,16]{0,1:T(8,128)} %param.17) | copy-start | bytes 6148
  180.8 7.0 %copy-start.3 = (s32[4,2]{0,1:T(2,128)S(1)}, s32[4,2]{0,1:T(2,128)}, u32[]{:S(2)}) copy-start(s32[4,2]{0,1:T(2,128)} %param.16) | copy-start | bytes 100
  211.1 53.7 %all-to-all-start = ((bf16[4,32,128,128]{3,2,0,1:T(8,128)(2,1)}), bf16[4,32,128,128]{3,2,0,1:T(8,128)(2,1)}, u32[]{:S(2)}, u32[]{:S(2)}) async-start(bf16[4,32,128,128]{3,2,0,1:T(8,128)(2,1)} %select_bitcast_fusion.1), calls=%async_computation.1 | async-start | bytes 8388608 | tf_op jit(solution)/shard_map/all_to_all | solution.py:96
Sparse Core Ops, SparseCore 0:
  187.7 147.1 reduce-scatter.1
where the time goes:
time: 346 us; the launch traced here: 344 us
  matrix products  87.7 us (25%)
  waiting for transfers between devices  85.9 us (25%)
  other arithmetic  70.1 us (20%)
  local copies, waits for them, and re-layouts  68.4 us (20%)
  between operations  14.2 us (4%)
  blocking collectives  10.3 us (3%)
  starting transfers between devices  4.64 us (1%)
    all_to_all x1, waiting for transfers between devices, per_device(): lax.all_to_all(outgoing, ('group', 'dp'), split_axis=1, concat_axis=1, ti...  46.2 us
    reduce_sum x4, other arithmetic, attend(): jnp.sum(expo, axis=-1, keepdims=True)  40.7 us
    reduce_scatter x1, waiting for transfers between devices, per_device(): lax.psum_scatter(jnp.dot(attn, w_out, preferred_element_type=jnp.float32)...  39.7 us
    dot_general x4, matrix products, attend(): jnp.einsum('kgct,tkd->ckgd', weights, pairs[:, :, 1], preferred_element_t...  36.2 us
    dot_general x4, matrix products, attend(): jnp.einsum('ckgd,tkd->kgct', query_p, pairs[:, :, 0], preferred_element_t...  35.9 us
    unnamed x13, local copies, waits for them, and re-layouts  14.1 us
    all_gather x1, blocking collectives, per_device(): lengths_every = lax.all_gather(lengths, ('group', 'dp'), axis=0, tiled=True)  10.3 us
    select_n x4, other arithmetic, attend(): jnp.where(key_pos < window, (key_pos >= window - history) & (key_pos >= q...  8.15 us
  transfers between devices with their start and end apart: 2, of which 2 were waited for; matrix products, arithmetic and copies ran while one was open for 13% of the time, Pallas kernels for 0%

commit v1 on v0

--- a/solution.py
+++ b/solution.py
@@ -4,6 +4,22 @@
 from jax.sharding import PartitionSpec as P
 
 HD = 64
+
+
+def gather_around(x, axis, dim):
+    ways, here, step = (lax.axis_size(axis), lax.axis_index(axis), x.shape[dim])
+    shape = [n * ways if d == dim else n for d, n in enumerate(x.shape)]
+    full = lax.dynamic_update_slice_in_dim(jnp.zeros(shape, x.dtype), x, here * step, axis=dim)
+    going_up = going_down = x
+    for far in range(1, ways // 2 + 1):
+        going_up = lax.ppermute(going_up, axis, [(d, (d + 1) % ways) for d in range(ways)])
+        full = lax.dynamic_update_slice_in_dim(full, going_up, (here - far) % ways * step, axis=dim)
+        if 2 * far < ways:
+            going_down = lax.ppermute(going_down, axis, [(d, (d - 1) % ways) for d in range(ways)])
+            full = lax.dynamic_update_slice_in_dim(
+                full, going_down, (here + far) % ways * step, axis=dim
+            )
+    return full
 
 
 def per_device(tokens, norm_gain, w_query, w_keyval, w_out, kv_cache, lengths, dest_slot):
@@ -78,7 +94,7 @@
     own_recv = lax.dynamic_index_in_dim(recv_all, my_index, 0, keepdims=False)
     senders = jnp.arange(devices, dtype=jnp.int32)[:, None]
     capacity = per_peer // 2
-    lengths_every = lax.all_gather(lengths, ("group", "dp"), axis=0, tiled=True)
+    lengths_every = gather_around(lengths, ("group", "dp"), 0)
     live_all = (
         (jnp.arange(blocks_win)[None, :] + 1) * block_len > window - lengths_every[:, 0:1]
     ).reshape(devices, per_dev)

time: 346 us -> 346 us (level)
  blocking collectives: 10.3 us -> 0 us
  starting transfers between devices: 4.64 us -> 13.3 us
    all_gather x1 -> x0, blocking collectives: 10.3 us -> none  [per_device(): lengths_every = lax.all_gather(lengths, ('group', 'dp'), axis=0, tiled=True)]
    ppermute x0 -> x7, starting transfers between devices: none -> 8.65 us  [the longest x3 8.13 us: gather_around(): lax.ppermute(going_down, axis, [(d, (d - 1) % ways) for d in range(ways)])]
    ppermute x0 -> x7, waiting for transfers between devices: none -> 5.99 us  [the longest x4 5.77 us: gather_around(): lax.ppermute(going_up, axis, [(d, (d + 1) % ways) for d in range(ways)])]
    reduce_scatter x1, waiting for transfers between devices: 39.7 us -> 34.1 us  [per_device(): lax.psum_scatter(jnp.dot(attn, w_out, preferred_element_type=jnp.float32)...]
    unnamed x13 -> x12, local copies, waits for them, and re-layouts: 14.1 us -> 14 us
  transfers between devices with their start and end apart: 2 -> 9, of which waited for: 2 -> 8; matrix products, arithmetic and copies ran while one was open for 13% -> 14% of each run, Pallas kernels for 0% -> 0%
where the time goes in v1:
time: 346 us; the launch traced here: 344 us
  matrix products  87.7 us (25%)
  waiting for transfers between devices  86.3 us (25%)
  other arithmetic  70.2 us (20%)
  local copies, waits for them, and re-layouts  69.7 us (20%)
  between operations  14.3 us (4%)
  starting transfers between devices  13.3 us (4%)
    all_to_all x1, waiting for transfers between devices, per_device(): lax.all_to_all(outgoing, ('group', 'dp'), split_axis=1, concat_axis=1, ti...  46.2 us
    reduce_sum x4, other arithmetic, attend(): jnp.sum(expo, axis=-1, keepdims=True)  40.7 us
    dot_general x4, matrix products, attend(): jnp.einsum('kgct,tkd->ckgd', weights, pairs[:, :, 1], preferred_element_t...  36.2 us
    dot_general x4, matrix products, attend(): jnp.einsum('ckgd,tkd->kgct', query_p, pairs[:, :, 0], preferred_element_t...  35.9 us
    reduce_scatter x1, waiting for transfers between devices, per_device(): lax.psum_scatter(jnp.dot(attn, w_out, preferred_element_type=jnp.float32)...  34.1 us
    unnamed x12, local copies, waits for them, and re-layouts  14 us
    select_n x4, other arithmetic, attend(): jnp.where(key_pos < window, (key_pos >= window - history) & (key_pos >= q...  8.15 us
    ppermute x3, starting transfers between devices, gather_around(): lax.ppermute(going_down, axis, [(d, (d - 1) % ways) for d in range(ways)])  8.13 us
  transfers between devices with their start and end apart: 9, of which 8 were waited for; matrix products, arithmetic and copies ran while one was open for 14% of the time, Pallas kernels for 0%

profile of v1, /device:TPU:0, one launch (start us, length us, event | category | flops | bytes accessed | tf_op | source)
XLA Modules:
  0.0 344.5 jit_solution(14722037447266665043)
XLA Ops:
  7.2 1.4 slice_bitcast_fusion
  8.6 3.2 slice.25
  11.8 4.5 %copy.36 = bf16[1,4,16,128,128]{3,2,4,1,0:T(8,128)(2,1)} copy(bf16[1,4,16,128,128]{4,3,2,1,0:T(8,128)(2,1)} %slice.25) | data formatting | bytes 4194304 | tf_op jit(solution)/shard_map/slice | solution.py:47
  16.3 4.2 %reshape_squeeze.3 = bf16[4,2048,1,2,64]{1,4,3,2,0:T(8,128)(2,1)} reshape(bf16[1,4,16,128,128]{3,2,4,1,0:T(8,128)(2,1)} %copy.36) | data formatting | bytes 4194304 | tf_op jit(solution)/shard_map/reshape;squeeze | solution.py:47
  20.4 3.1 fusion.27
  23.5 3.6 %fusion.33 = bf16[1024,128]{1,0:T(8,128)(2,1)S(1)} fusion(bf16[2048,128]{1,0:T(8,128)(2,1)} %param.13, bf16[1024,2048]{1,0:T(8,128)(2,1)} %param.10, f32[2048]{0:T(1024)S(1)} %convert_element_type.40, f32[1024]{0:T(1024)S(1)} %add_rsqrt_fusion), kind=kOutput, calls=%fused_computation.51 | convolution fusion | flops 545390592 | bytes 4993024 | tf_op jit(solution)/shard_map/dot_general | solution.py:45
  27.7 5.3 %convolution_convert_fusion = bf16[1024,512]{1,0:T(8,128)(2,1)S(1)} fusion(bf16[2048,512]{1,0:T(8,128)(2,1)} %param.12, bf16[1024,2048]{1,0:T(8,128)(2,1)} %param.10, f32[2048]{0:T(1024)S(1)} %convert_element_type.40, f32[1024]{0:T(1024)S(1)} %add_rsqrt_fusion), kind=kOutput, calls=%fused_computation.49 | convolution fusion | flops 2156396544 | bytes 7352320 | tf_op jit(solution)/shard_map/dot_general | solution.py:43
  33.0 2.1 reshape.479
  35.1 3.0 copy.40
  38.1 142.6 %while.14 = (s32[]{:T(128)}, bf16[4,256,512]{2,1,0:T(8,128)(2,1)}, s32[4]{0:T(128)}, bf16[4,2048,1,2,64]{1,4,3,2,0:T(8,128)(2,1)}, bf16[4,256,1,2,64]{1,4,3,2,0:...) while((s32[]{:T(128)}, bf16[4,256,512]{2,1,0:T(8,128)(2,1)}, ...), condition=%wide.region_4.5_spmd.clone.clone, body=%wide.region_1.4_spmd.clone.clone.sunk | while | flops 1268387072 | bytes 63510268 | solution.py:78
  38.1 1.3 dynamic_slice.91
  40.1 2.0 fusion.58
  42.2 1.1 dynamic-slice_bitcast_fusion.5
  43.3 9.0 %fusion.59 = (f32[8,256]{1,0:T(8,128)S(1)}, f32[2304,256,8]{1,0,2:T(8,128)}) fusion(pred[256,2304]{0,1:T(8,128)(4,1)S(1)} %fusion.58, bf16[4,256,1,8,64]{1,4,3,2,0:T(8,128)(2,1)} %get-tuple-element.301, s32[]{:T(128)S(6)} %copy.58, bf16[256,1,2,64]{0,3,2,1:T(8,128)(2,1)S(1)} %dynamic-slice_bitcast_fusion.4, ...), kind=kOutput, calls=%fused_computation.10.clone.1 | convolution fusion | flops 618723328 | bytes 20324356 | tf_op jit(solution)/shard_map/while/body/eval_jaxpr/ckgd,tkd->kgct/dot_general | solution.py:56
  52.3 10.2 %fusion.60 = f32[8,256]{1,0:T(8,128)S(1)} fusion(f32[2304,256,8]{1,0,2:T(8,128)} %get-tuple-element.275, f32[8,256]{1,0:T(8,128)S(1)} %get-tuple-element.276, pred[256,2304]{0,1:T(8,128)(4,1)S(1)} %fusion.58), kind=kLoop, calls=%fused_computation.9.clone.1 | loop fusion | flops 18872320 | bytes 19480576 | tf_op jit(solution)/shard_map/while/body/eval_jaxpr/reduce_sum | solution.py:69
  62.5 9.0 %fusion.61 = bf16[64,8,256]{2,0,1:T(8,128)(2,1)S(1)} fusion(f32[8,256]{1,0:T(8,128)S(1)} %fusion.60, f32[8,256]{1,0:T(8,128)S(1)} %get-tuple-element.276, f32[2304,256,8]{1,0,2:T(8,128)} %get-tuple-element.275, pred[256,2304]{0,1:T(8,128)(4,1)S(1)} %fusion.58, bf16[2048,1,2,64]{0,3,2,1:T(8,128)(2,1)S(1)} %dynamic-slice_bitcast_fusion.5, ...), kind=kOutput, calls=%fused_computation.17.clone.1 | convolution fusion | flops 628293632 | bytes 20332544 | tf_op jit(solution)/shard_map/while/body/eval_jaxpr/kgct,tkd->ckgd/dot_general | solution.py:70
  73.8 1.3 dynamic_slice.91
  75.8 2.0 fusion.58
  77.9 1.1 dynamic-slice_bitcast_fusion.5
  78.9 9.0 %fusion.59 = (f32[8,256]{1,0:T(8,128)S(1)}, f32[2304,256,8]{1,0,2:T(8,128)}) fusion(pred[256,2304]{0,1:T(8,128)(4,1)S(1)} %fusion.58, bf16[4,256,1,8,64]{1,4,3,2,0:T(8,128)(2,1)} %get-tuple-element.301, s32[]{:T(128)S(6)} %copy.58, bf16[256,1,2,64]{0,3,2,1:T(8,128)(2,1)S(1)} %dynamic-slice_bitcast_fusion.4, ...), kind=kOutput, calls=%fused_computation.10.clone.1 | convolution fusion | flops 618723328 | bytes 20324356 | tf_op jit(solution)/shard_map/while/body/eval_jaxpr/ckgd,tkd->kgct/dot_general | solution.py:56
  87.9 10.2 %fusion.60 = f32[8,256]{1,0:T(8,128)S(1)} fusion(f32[2304,256,8]{1,0,2:T(8,128)} %get-tuple-element.275, f32[8,256]{1,0:T(8,128)S(1)} %get-tuple-element.276, pred[256,2304]{0,1:T(8,128)(4,1)S(1)} %fusion.58), kind=kLoop, calls=%fused_computation.9.clone.1 | loop fusion | flops 18872320 | bytes 19480576 | tf_op jit(solution)/shard_map/while/body/eval_jaxpr/reduce_sum | solution.py:69
  98.1 9.0 %fusion.61 = bf16[64,8,256]{2,0,1:T(8,128)(2,1)S(1)} fusion(f32[8,256]{1,0:T(8,128)S(1)} %fusion.60, f32[8,256]{1,0:T(8,128)S(1)} %get-tuple-element.276, f32[2304,256,8]{1,0,2:T(8,128)} %get-tuple-element.275, pred[256,2304]{0,1:T(8,128)(4,1)S(1)} %fusion.58, bf16[2048,1,2,64]{0,3,2,1:T(8,128)(2,1)S(1)} %dynamic-slice_bitcast_fusion.5, ...), kind=kOutput, calls=%fused_computation.17.clone.1 | convolution fusion | flops 628293632 | bytes 20332544 | tf_op jit(solution)/shard_map/while/body/eval_jaxpr/kgct,tkd->ckgd/dot_general | solution.py:70
  109.5 1.3 dynamic_slice.91
  111.4 2.0 fusion.58
  114.6 9.0 %fusion.59 = (f32[8,256]{1,0:T(8,128)S(1)}, f32[2304,256,8]{1,0,2:T(8,128)}) fusion(pred[256,2304]{0,1:T(8,128)(4,1)S(1)} %fusion.58, bf16[4,256,1,8,64]{1,4,3,2,0:T(8,128)(2,1)} %get-tuple-element.301, s32[]{:T(128)S(6)} %copy.58, bf16[256,1,2,64]{0,3,2,1:T(8,128)(2,1)S(1)} %dynamic-slice_bitcast_fusion.4, ...), kind=kOutput, calls=%fused_computation.10.clone.1 | convolution fusion | flops 618723328 | bytes 20324356 | tf_op jit(solution)/shard_map/while/body/eval_jaxpr/ckgd,tkd->kgct/dot_general | solution.py:56
  123.6 10.2 %fusion.60 = f32[8,256]{1,0:T(8,128)S(1)} fusion(f32[2304,256,8]{1,0,2:T(8,128)} %get-tuple-element.275, f32[8,256]{1,0:T(8,128)S(1)} %get-tuple-element.276, pred[256,2304]{0,1:T(8,128)(4,1)S(1)} %fusion.58), kind=kLoop, calls=%fused_computation.9.clone.1 | loop fusion | flops 18872320 | bytes 19480576 | tf_op jit(solution)/shard_map/while/body/eval_jaxpr/reduce_sum | solution.py:69
  133.8 9.0 %fusion.61 = bf16[64,8,256]{2,0,1:T(8,128)(2,1)S(1)} fusion(f32[8,256]{1,0:T(8,128)S(1)} %fusion.60, f32[8,256]{1,0:T(8,128)S(1)} %get-tuple-element.276, f32[2304,256,8]{1,0,2:T(8,128)} %get-tuple-element.275, pred[256,2304]{0,1:T(8,128)(4,1)S(1)} %fusion.58, bf16[2048,1,2,64]{0,3,2,1:T(8,128)(2,1)S(1)} %dynamic-slice_bitcast_fusion.5, ...), kind=kOutput, calls=%fused_computation.17.clone.1 | convolution fusion | flops 628293632 | bytes 20332544 | tf_op jit(solution)/shard_map/while/body/eval_jaxpr/kgct,tkd->ckgd/dot_general | solution.py:70
  145.1 1.3 dynamic_slice.91
  147.1 2.0 fusion.58
  150.2 9.0 %fusion.59 = (f32[8,256]{1,0:T(8,128)S(1)}, f32[2304,256,8]{1,0,2:T(8,128)}) fusion(pred[256,2304]{0,1:T(8,128)(4,1)S(1)} %fusion.58, bf16[4,256,1,8,64]{1,4,3,2,0:T(8,128)(2,1)} %get-tuple-element.301, s32[]{:T(128)S(6)} %copy.58, bf16[256,1,2,64]{0,3,2,1:T(8,128)(2,1)S(1)} %dynamic-slice_bitcast_fusion.4, ...), kind=kOutput, calls=%fused_computation.10.clone.1 | convolution fusion | flops 618723328 | bytes 20324356 | tf_op jit(solution)/shard_map/while/body/eval_jaxpr/ckgd,tkd->kgct/dot_general | solution.py:56
  159.2 10.2 %fusion.60 = f32[8,256]{1,0:T(8,128)S(1)} fusion(f32[2304,256,8]{1,0,2:T(8,128)} %get-tuple-element.275, f32[8,256]{1,0:T(8,128)S(1)} %get-tuple-element.276, pred[256,2304]{0,1:T(8,128)(4,1)S(1)} %fusion.58), kind=kLoop, calls=%fused_computation.9.clone.1 | loop fusion | flops 18872320 | bytes 19480576 | tf_op jit(solution)/shard_map/while/body/eval_jaxpr/reduce_sum | solution.py:69
  169.4 9.0 %fusion.61 = bf16[64,8,256]{2,0,1:T(8,128)(2,1)S(1)} fusion(f32[8,256]{1,0:T(8,128)S(1)} %fusion.60, f32[8,256]{1,0:T(8,128)S(1)} %get-tuple-element.276, f32[2304,256,8]{1,0,2:T(8,128)} %get-tuple-element.275, pred[256,2304]{0,1:T(8,128)(4,1)S(1)} %fusion.58, bf16[2048,1,2,64]{0,3,2,1:T(8,128)(2,1)S(1)} %dynamic-slice_bitcast_fusion.5, ...), kind=kOutput, calls=%fused_computation.17.clone.1 | convolution fusion | flops 628293632 | bytes 20332544 | tf_op jit(solution)/shard_map/while/body/eval_jaxpr/kgct,tkd->ckgd/dot_general | solution.py:70
  180.8 6.8 %fusion.45 = f32[1024,2048]{1,0:T(8,128)} fusion(bf16[1024,512]{1,0:T(8,128)(2,1)} %bitcast.98, bf16[512,2048]{1,0:T(8,128)(2,1)S(1)} %copy-done), kind=kOutput, calls=%fused_computation.92 | convolution fusion | flops 2147483648 | bytes 11534336 | tf_op jit(solution)/shard_map/dot_general | solution.py:81
  188.1 2.9 collective-permute-start.1
  192.4 2.6 collective-permute-start.3
  196.3 2.6 collective-permute-start.5
  200.5 3.4 %collective-permute-done.6 = s32[4,2]{0,1:T(2,128)S(1)} collective-permute-done((s32[4,2]{0,1:T(2,128)S(1)}, s32[4,2]{0,1:T(2,128)S(1)}, u32[]{:S(2)}, u32[]{:S(2)}) %collective-permute-start.6) | collective-permute-done | bytes 64 | tf_op jit(solution)/shard_map/ppermute | solution.py:15
  205.6 6.5 %gather_fusion = bf16[32,4,128,128]{3,2,1,0:T(8,128)(2,1)} fusion(bf16[4,64,128,128]{3,2,1,0:T(8,128)(2,1)} %bitcast.96, s32[1024]{0:T(1024)S(1)} %pad_clamp_fusion.1), kind=kCustom, calls=%fused_computation | custom fusion | bytes 8388736 | tf_op jit(solution)/shard_map/jit(_take)/gather | solution.py:111
  212.1 4.7 %select_bitcast_fusion.1 = bf16[4,32,128,128]{3,2,0,1:T(8,128)(2,1)} fusion(bf16[32,4,128,128]{3,2,1,0:T(8,128)(2,1)} %gather_fusion, pred[32]{0:T(512)(128)(4,1)S(1)} %compare_and_fusion), kind=kLoop, calls=%fused_computation.48 | loop fusion | flops 2097152 | bytes 8388640 | tf_op jit(solution)/shard_map/jit(_take)/select_n | solution.py:111
  216.8 4.6 %all-to-all-start = ((bf16[4,32,128,128]{3,2,0,1:T(8,128)(2,1)}), bf16[4,32,128,128]{3,2,0,1:T(8,128)(2,1)}, u32[]{:S(2)}, u32[]{:S(2)}) async-start(bf16[4,32,128,128]{3,2,0,1:T(8,128)(2,1)} %select_bitcast_fusion.1), calls=%async_computation.1 | async-start | bytes 8388608 | tf_op jit(solution)/shard_map/all_to_all | solution.py:112
  221.8 2.4 scatter_custom_fusion
  224.3 46.2 %all-to-all-done = bf16[4,32,128,128]{3,2,0,1:T(8,128)(2,1)} async-done(((bf16[4,32,128,128]{3,2,0,1:T(8,128)(2,1)}), bf16[4,32,128,128]{3,2,0,1:T(8,128)(2,1)}, u32[]{:S(2)}, u32[]{:S(2)}) %all-to-all-start) | async-done | bytes 4194336 | tf_op jit(solution)/shard_map/all_to_all | solution.py:112
  270.5 4.7 %copy.44 = bf16[4,32,128,128]{3,2,1,0:T(8,128)(2,1)} copy(bf16[4,32,128,128]{3,2,0,1:T(8,128)(2,1)} %all-to-all-done) | data formatting | bytes 8388608 | tf_op jit(solution)/shard_map/all_to_all | solution.py:112
  275.2 7.8 %gather_fusion.1 = bf16[64,4,128,128]{3,2,1,0:T(8,128)(2,1)} fusion(bf16[4,32,128,128]{3,2,1,0:T(8,128)(2,1)} %copy.44, s32[1024]{0:T(1024)S(1)} %pad_clamp_fusion), kind=kCustom, calls=%fused_computation.1 | custom fusion | bytes 16777472 | tf_op jit(solution)/shard_map/jit(_take)/gather | solution.py:121
  283.0 7.3 %select_bitcast_fusion = bf16[4,64,128,128]{3,2,0,1:T(8,128)(2,1)} fusion(bf16[64,4,128,128]{3,2,1,0:T(8,128)(2,1)} %gather_fusion.1, pred[64]{0:T(512)(128)(4,1)S(1)} %compare_and_fusion.1), kind=kLoop, calls=%fused_computation.47 | loop fusion | flops 4194304 | bytes 16777280 | tf_op jit(solution)/shard_map/jit(_take)/select_n | solution.py:121
  290.3 10.5 %copy.45 = bf16[4,64,128,128]{3,2,1,0:T(8,128)(2,1)} copy(bf16[4,64,128,128]{3,2,0,1:T(8,128)(2,1)} %select_bitcast_fusion) | data formatting | bytes 16777216
  300.9 34.1 %reduce-scatter.2.cloned.1.call-done = f32[256,2048]{1,0:T(8,128)} async-done(((f32[1024,2048]{1,0:T(8,128)}), f32[256,2048]{1,0:T(8,128)}) %reduce-scatter.2.cloned.1.call-update) | async-done | bytes 2097168 | tf_op jit(solution)/shard_map/reduce_scatter | solution.py:80
  334.9 2.7 convert_element_type.44
  (110 shorter events, 18.7 us)
Async XLA Ops:
  7.2 173.6 %copy-start = (bf16[512,2048]{1,0:T(8,128)(2,1)S(1)}, bf16[512,2048]{1,0:T(8,128)(2,1)}, u32[]{:S(2)}) copy-start(bf16[512,2048]{1,0:T(8,128)(2,1)} %param.14) | copy-start | bytes 6291460
  7.2 13.2 %copy-start.2 = (bf16[2048]{0:T(1024)(128)(2,1)S(1)}, bf16[2048]{0:T(1024)(128)(2,1)}, u32[]{:S(2)}) copy-start(bf16[2048]{0:T(1024)(128)(2,1)} %param.11) | copy-start | bytes 12292
  7.2 327.7 %reduce-scatter.2.cloned.1.call-start = ((), (), s32[]{:S(2)}) async-start(), calls=%async_computation.2 | async-start | bytes 10485760 | tf_op jit(solution)/shard_map/reduce_scatter | solution.py:80
  62.4 9.1 %copy-start.4 = (s32[4]{0:T(128)S(1)}, s32[4]{0:T(128)}, u32[]{:S(2)}) copy-start(s32[4]{0:T(128)} %get-tuple-element.297) | copy-start | bytes 52 | tf_op jit(solution)/shard_map/while
  98.1 9.1 %copy-start.4 = (s32[4]{0:T(128)S(1)}, s32[4]{0:T(128)}, u32[]{:S(2)}) copy-start(s32[4]{0:T(128)} %get-tuple-element.297) | copy-start | bytes 52 | tf_op jit(solution)/shard_map/while
  133.8 9.1 %copy-start.4 = (s32[4]{0:T(128)S(1)}, s32[4]{0:T(128)}, u32[]{:S(2)}) copy-start(s32[4]{0:T(128)} %get-tuple-element.297) | copy-start | bytes 52 | tf_op jit(solution)/shard_map/while
  169.4 9.1 %copy-start.4 = (s32[4]{0:T(128)S(1)}, s32[4]{0:T(128)}, u32[]{:S(2)}) copy-start(s32[4]{0:T(128)} %get-tuple-element.297) | copy-start | bytes 52 | tf_op jit(solution)/shard_map/while
  180.8 6.8 %copy-start.3 = (s32[4,2]{0,1:T(2,128)S(1)}, s32[4,2]{0,1:T(2,128)}, u32[]{:S(2)}) copy-start(s32[4,2]{0,1:T(2,128)} %param.16) | copy-start | bytes 100
  180.8 10.3 %copy-start.1 = (s32[32,16]{0,1:T(8,128)S(1)}, s32[32,16]{0,1:T(8,128)}, u32[]{:S(2)}) copy-start(s32[32,16]{0,1:T(8,128)} %param.17) | copy-start | bytes 6148
  187.6 4.6 %collective-permute-start = (s32[4,2]{0,1:T(2,128)S(1)}, s32[4,2]{0,1:T(2,128)S(1)}, u32[]{:S(2)}, u32[]{:S(2)}) collective-permute-start(s32[4,2]{0,1:T(2,128)S(1)} %copy-done.3), channel_id=1, source_target_pairs={{0,4},{4,8},{8,12},{12,16},{16,20},{20,24},{24,28},{28,0},{1,5},{5... | collective-permute-start | bytes 104 | tf_op jit(solution)/shard_map/ppermute | solution.py:15
  188.1 4.2 %collective-permute-start.1 = (s32[4,2]{0,1:T(2,128)S(1)}, s32[4,2]{0,1:T(2,128)S(1)}, u32[]{:S(2)}, u32[]{:S(2)}) collective-permute-start(s32[4,2]{0,1:T(2,128)S(1)} %copy-done.3), channel_id=1, source_target_pairs={{0,28},{4,0},{8,4},{12,8},{16,12},{20,16},{24,20},{28,24},{1,29},{... | collective-permute-start | bytes 104 | tf_op jit(solution)/shard_map/ppermute | solution.py:18
  192.3 3.9 %collective-permute-start.2 = (s32[4,2]{0,1:T(2,128)S(1)}, s32[4,2]{0,1:T(2,128)S(1)}, u32[]{:S(2)}, u32[]{:S(2)}) collective-permute-start(s32[4,2]{0,1:T(2,128)S(1)} %collective-permute-done), channel_id=1, source_target_pairs={{0,4},{4,8},{8,12},{12,16},{16,20},{20,24},{24,28},{28,0},{1,5},{5... | collective-permute-start | bytes 104 | tf_op jit(solution)/shard_map/ppermute | solution.py:15
  192.4 3.9 %collective-permute-start.3 = (s32[4,2]{0,1:T(2,128)S(1)}, s32[4,2]{0,1:T(2,128)S(1)}, u32[]{:S(2)}, u32[]{:S(2)}) collective-permute-start(s32[4,2]{0,1:T(2,128)S(1)} %collective-permute-done.1), channel_id=1, source_target_pairs={{0,28},{4,0},{8,4},{12,8},{16,12},{20,16},{24,20},{28,24},{1,29},{... | collective-permute-start | bytes 104 | tf_op jit(solution)/shard_map/ppermute | solution.py:18
  196.2 3.9 %collective-permute-start.4 = (s32[4,2]{0,1:T(2,128)S(1)}, s32[4,2]{0,1:T(2,128)S(1)}, u32[]{:S(2)}, u32[]{:S(2)}) collective-permute-start(s32[4,2]{0,1:T(2,128)S(1)} %collective-permute-done.2), channel_id=1, source_target_pairs={{0,4},{4,8},{8,12},{12,16},{16,20},{20,24},{24,28},{28,0},{1,5},{5... | collective-permute-start | bytes 104 | tf_op jit(solution)/shard_map/ppermute | solution.py:15
  196.3 4.0 %collective-permute-start.5 = (s32[4,2]{0,1:T(2,128)S(1)}, s32[4,2]{0,1:T(2,128)S(1)}, u32[]{:S(2)}, u32[]{:S(2)}) collective-permute-start(s32[4,2]{0,1:T(2,128)S(1)} %collective-permute-done.3), channel_id=1, source_target_pairs={{0,28},{4,0},{8,4},{12,8},{16,12},{20,16},{24,20},{28,24},{1,29},{... | collective-permute-start | bytes 104 | tf_op jit(solution)/shard_map/ppermute | solution.py:18
  200.0 3.9 %collective-permute-start.6 = (s32[4,2]{0,1:T(2,128)S(1)}, s32[4,2]{0,1:T(2,128)S(1)}, u32[]{:S(2)}, u32[]{:S(2)}) collective-permute-start(s32[4,2]{0,1:T(2,128)S(1)} %collective-permute-done.4), channel_id=1, source_target_pairs={{0,4},{4,8},{8,12},{12,16},{16,20},{20,24},{24,28},{28,0},{1,5},{5... | collective-permute-start | bytes 104 | tf_op jit(solution)/shard_map/ppermute | solution.py:15
  216.8 53.7 %all-to-all-start = ((bf16[4,32,128,128]{3,2,0,1:T(8,128)(2,1)}), bf16[4,32,128,128]{3,2,0,1:T(8,128)(2,1)}, u32[]{:S(2)}, u32[]{:S(2)}) async-start(bf16[4,32,128,128]{3,2,0,1:T(8,128)(2,1)} %select_bitcast_fusion.1), calls=%async_computation.1 | async-start | bytes 8388608 | tf_op jit(solution)/shard_map/all_to_all | solution.py:112
Sparse Core Ops, SparseCore 0:
  187.7 147.1 reduce-scatter.1
